TPU v7x, 256 devices: a whole 4x4x8 slice. The times are simulated.
256 devices in a mesh: group: 8 (over x, z_lo), replica: 32 (over y, z_hi, core).
Axes of the slice: x: 4, y: 4, z: 8 (z_hi: 4, z_lo: 2; z = z_hi * 2 + z_lo), core: 2. Of those that a mesh axis runs over, the one named last changes fastest.
Arguments:
- hidden_in: bfloat16 [81920, 3072], P(('group', 'replica')), may hold values from -24 to 24
- w_query: bfloat16 [3072, 1536], replicated, may hold values from -0.109375 to 0.109375
- query_gain: float32 [128], replicated, may hold values from 0.5 to 2
- down_projection_matrix: bfloat16 [3072, 64], replicated, may hold values from -0.23925781 to 0.23925781
- up_projection_matrix: bfloat16 [64, 1536], replicated, may hold values from -0.59765625 to 0.59765625
- query_cotangent: bfloat16 [81920, 1536], P(('group', 'replica')), may hold values from -24 to 24
- first_moment: float32 [4608, 64], P(('group', 'replica')), may hold values from -3 to 3
- second_moment: float32 [4608, 64], P(('group', 'replica')), may hold values from 0.001 to 0.1
Outputs:
- new_down: bfloat16 [3072, 64], replicated
- new_up: bfloat16 [64, 1536], replicated
- first_next: float32 [4608, 64], P(('group', 'replica'))
- second_next: float32 [4608, 64], P(('group', 'replica'))
All inputs are finite; a program needn't handle non-finite values.
Results may differ from a plain program's by a relative error of at most 0.0019.
Values may be sent and summed in bfloat16 or wider, within the bound.
A program may use at most 64 MiB of HBM per device.

v0:
```python
import jax
import jax.numpy as jnp
from jax import lax
from jax.sharding import PartitionSpec as P

adapter_scale_factor = 0.5
norm_epsilon = 1e-06
beta_one = 0.9
beta_two = 0.999
first_bias = 1.0 - 0.9**10
second_bias = 1.0 - 0.999**10
learn_rate = 0.001
adam_eps = 1e-08


def queries_backward(
    rows_in, grads_in, w_query, query_gain, down_projection_matrix, up_projection_matrix
):
    reduced_rank_input = jnp.dot(
        rows_in, down_projection_matrix, preferred_element_type=jnp.float32
    ).astype(jnp.bfloat16)
    apply_projection = jnp.dot(rows_in, w_query, preferred_element_type=jnp.float32)
    apply_projection = apply_projection + adapter_scale_factor * jnp.dot(
        reduced_rank_input, up_projection_matrix, preferred_element_type=jnp.float32
    )
    token_count = apply_projection.shape[0]
    head_size = query_gain.shape[0]
    shaped = apply_projection.reshape(token_count, -1, head_size)
    inverse = lax.rsqrt(jnp.mean(shaped * shaped, axis=-1, keepdims=True) + norm_epsilon)
    normed = shaped * inverse
    upstream = grads_in.astype(jnp.float32).reshape(shaped.shape) * query_gain
    grad_pre = inverse * (upstream - normed * jnp.mean(upstream * normed, axis=-1, keepdims=True))
    grad_pre = grad_pre.reshape(token_count, -1).astype(jnp.bfloat16)
    backward_reduced = lax.dot_general(
        grad_pre, up_projection_matrix, (((1,), (1,)), ((), ())), preferred_element_type=jnp.float32
    )
    backward_reduced = (adapter_scale_factor * backward_reduced).astype(jnp.bfloat16)
    scaled_reduced = (reduced_rank_input.astype(jnp.float32) * adapter_scale_factor).astype(
        jnp.bfloat16
    )
    return (grad_pre, backward_reduced, scaled_reduced)


def adam_update(grads, params, first, second):
    first_new = beta_one * first + (1.0 - beta_one) * grads
    second_new = beta_two * second + (1.0 - beta_two) * grads * grads
    direction = first_new / first_bias / (jnp.sqrt(second_new / second_bias) + adam_eps)
    return ((params - learn_rate * direction).astype(jnp.bfloat16), first_new, second_new)


def on_device(
    hidden_in,
    w_query,
    query_gain,
    down_projection_matrix,
    up_projection_matrix,
    query_cotangent,
    first_moment,
    second_moment,
):
    model_width = hidden_in.shape[1]
    adapter_rank_size = down_projection_matrix.shape[1]
    row_count_total = model_width + up_projection_matrix.shape[1]
    accelerator_list = lax.axis_size("group") * lax.axis_size("replica")
    own_rows = row_count_total // accelerator_list
    grad_pre, backward_reduced, scaled_reduced = queries_backward(
        hidden_in,
        query_cotangent,
        w_query,
        query_gain,
        down_projection_matrix,
        up_projection_matrix,
    )
    stacked = jnp.concatenate([hidden_in, grad_pre], axis=1)
    operand = jnp.concatenate([backward_reduced, scaled_reduced], axis=1)
    matrix_product = lax.dot_general(
        stacked, operand, (((0,), (0,)), ((), ())), preferred_element_type=jnp.float32
    )
    row_ids = lax.iota(jnp.int32, lax.axis_size(("group", "replica")) * own_rows)
    is_down_matrix = (row_ids < model_width)[:, None]
    grad_own = lax.psum_scatter(
        jnp.where(
            is_down_matrix,
            matrix_product[:, :adapter_rank_size],
            matrix_product[:, adapter_rank_size:],
        )
        / accelerator_list,
        ("group", "replica"),
        scatter_dimension=0,
        tiled=True,
    )
    owner = lax.axis_index(("group", "replica"))
    combined = jnp.concatenate([down_projection_matrix, up_projection_matrix.T], axis=0)
    params_own = lax.dynamic_slice_in_dim(combined, owner * own_rows, own_rows, 0).astype(
        jnp.float32
    )
    updated_own, first_new, second_new = adam_update(
        grad_own, params_own, first_moment, second_moment
    )
    gathered = lax.all_gather(updated_own, ("group", "replica"), axis=0, tiled=True)
    return (gathered[:model_width], gathered[model_width:].T, first_new, second_new)


def solution(mesh):
    placed = (
        P(("group", "replica"), None),
        P(),
        P(),
        P(),
        P(),
        P(("group", "replica"), None),
        P(("group", "replica"), None),
        P(("group", "replica"), None),
    )
    return jax.shard_map(
        on_device,
        mesh=mesh,
        in_specs=placed,
        out_specs=(P(), P(), P(("group", "replica"), None), P(("group", "replica"), None)),
        check_vma=False,
    )
```

profile of v0, /device:TPU:1, one launch (start us, length us, event | category | flops | bytes accessed | tf_op | source)
XLA Modules:
  0.0 660.7 jit_solution(2586570845125717426)
XLA Ops:
  7.2 0.0 copy-start.1
  7.2 0.0 all-reduce.3.cloned.1.call-start
  7.2 3.1 multiply_convert_fusion.1
  10.3 0.0 copy-done.1
  10.3 0.0 copy-start.4
  10.3 5.8 fusion.15
  16.1 0.0 copy-done.4
  16.1 1.7 fusion.4
  17.8 2.0 copy.42
  19.8 0.0 copy-start.3
  19.8 0.2 multiply_reduce_fusion.1
  20.0 0.6 add_rsqrt_fusion
  20.6 0.4 copy-done.3
  21.0 1.7 copy.44
  22.7 0.7 broadcast_bitcast_fusion
  23.4 2.2 multiply_reduce_fusion
  25.6 0.2 mul.117
  25.7 1.9 copy.45
  27.6 2.3 mul.106
  29.9 0.0 copy-start
  29.9 3.1 copy.46
  33.0 0.0 copy-done
  33.0 0.0 copy-start.2
  33.1 0.0 copy-start.6
  33.1 3.0 multiply_convert_fusion
  36.1 0.4 fusion.6
  36.5 0.0 copy-done.2
  36.5 0.0 copy-done.6
  36.5 0.8 fusion
  37.3 0.0 copy-start.5
  37.3 1.2 fusion.5
  38.5 0.0 copy-start.7
  38.5 0.0 copy-start.8
  38.5 0.0 all-reduce.3.cloned.1.call-update
  38.5 0.0 copy-done.5
  38.5 0.4 copy.41
  38.9 0.2 copy.40
  39.2 261.5 %all-reduce.3.cloned.1.call-done = f32[4608,64]{0,1:T(8,128)} async-done(((f32[4608,64]{0,1:T(8,128)}), f32[4608,64]{0,1:T(8,128)}) %all-reduce.3.cloned.1.call-update) | async-done | bytes 1179664
  300.7 0.9 constant_dynamic-slice_fusion
  301.6 0.1 copy.47
  301.6 0.0 copy-done.7
  301.6 0.0 copy-done.8
  301.7 0.6 fusion.12
  302.3 349.1 %all-gather = bf16[256,18,64]{2,1,0:T(8,128)(2,1)S(1)} all-gather(bf16[1,18,64]{2,1,0:T(8,128)(2,1)S(1)} %get-tuple-element.20), channel_id=1, replica_groups=mesh['group'=8,'replica'=32] {'group','replica'}, dimensions={0}, use_global_device_ids=true | all-gather | bytes 592128 | tf_op jit(solution)/shard_map/all_gather | solution.py:100
  651.4 0.6 reshape.39
  651.9 0.1 slice.18
  652.0 1.0 copy.50
  653.0 0.8 copy.51
  (3 shorter events, 0.0 us)
Async XLA Ops:
  7.2 3.1 copy-start.1
  7.2 293.5 %all-reduce.3.cloned.1.call-start = ((), (), s32[]{:S(2)}) async-start(), calls=%async_computation | async-start | bytes 2359296
  10.3 5.8 copy-start.4
  19.8 1.2 copy-start.3
  29.9 3.1 copy-start
  33.0 3.5 copy-start.2
  33.1 3.5 copy-start.6
  37.3 1.2 copy-start.5
  38.5 263.2 %copy-start.7 = (f32[18,64]{1,0:T(8,128)S(1)}, f32[18,64]{1,0:T(8,128)}, u32[]{:S(2)}) copy-start(f32[18,64]{1,0:T(8,128)} %param.14) | copy-start | bytes 13828
  38.5 263.2 %copy-start.8 = (f32[18,64]{1,0:T(8,128)S(1)}, f32[18,64]{1,0:T(8,128)}, u32[]{:S(2)}) copy-start(f32[18,64]{1,0:T(8,128)} %param.15) | copy-start | bytes 13828
Sparse Core Ops, SparseCore 0:
  38.6 261.9 all-reduce.2
where the time goes:
time: 661 us
  blocking collectives  349 us (53%)
  waiting for transfers between devices  262 us (40%)
  local copies, waits for them, and re-layouts  16.3 us (2%)
  between operations  14.2 us (2%)
  matrix products  11.7 us (2%)
  other arithmetic  7.86 us (1%)
    all_gather x1, blocking collectives, on_device(): lax.all_gather(updated_own, ('group', 'replica'), axis=0, tiled=True)  349 us
    unnamed x2, waiting for transfers between devices  262 us
  transfers between devices with their start and end apart: 1, of which 1 were waited for; matrix products, arithmetic and copies ran while one was open for 0% of the time, Pallas kernels for 0%

commit v1 on v0

--- a/solution.py
+++ b/solution.py
@@ -1,6 +1,10 @@
+import functools
+
 import jax
 import jax.numpy as jnp
 from jax import lax
+from jax.experimental import pallas as pl
+from jax.experimental.pallas import tpu as pltpu
 from jax.sharding import PartitionSpec as P
 
 adapter_scale_factor = 0.5
@@ -11,6 +15,12 @@
 second_bias = 1.0 - 0.999**10
 learn_rate = 0.001
 adam_eps = 1e-08
+
+MESH = pl.DeviceIdType.MESH
+NX, NY, NZH = 4, 4, 4
+OWN = 18
+HALF = 72
+N_DEV = 256
 
 
 def queries_backward(
@@ -46,6 +56,211 @@
     second_new = beta_two * second + (1.0 - beta_two) * grads * grads
     direction = first_new / first_bias / (jnp.sqrt(second_new / second_bias) + adam_eps)
     return ((params - learn_rate * direction).astype(jnp.bfloat16), first_new, second_new)
+
+
+def exchange_kernel(
+    p_ref, par_ref, m_ref, v_ref,
+    first_ref, second_ref, g_ref,
+    cbuf, qf, qb, xbuf, zsend, zbuf, ubuf, abuf, rows, gbuf,
+    cs, cr, xs, xr, zs, zr, us, ur, bs, br, fs, fr,
+):
+    g = lax.axis_index("group")
+    r = lax.axis_index("replica")
+    x, zl = g // 2, g % 2
+    y, zh, c = r // 8, (r // 2) % 4, r % 2
+    t_me = x * NY + y
+
+    def dev(x_, y_, zh_, zl_, c_):
+        return (x_ * 2 + zl_, y_ * 8 + zh_ * 2 + c_)
+
+    def rdma(src, dst, ssem, rsem, to):
+        return pltpu.make_async_remote_copy(
+            src_ref=src, dst_ref=dst, send_sem=ssem, recv_sem=rsem,
+            device_id=to, device_id_type=MESH)
+
+    partner = dev(x, y, zh, zl, 1 - c)
+
+    barrier = pltpu.get_barrier_semaphore()
+    for d in range(1, 16):
+        pl.semaphore_signal(
+            barrier, inc=1, device_id_type=MESH,
+            device_id=dev((x + d // 4) % NX, (y + d % 4) % NY, zh, zl, c))
+    for d in range(1, 16):
+        k = (zh * 4 + zl * 2 + c + d) % 16
+        pl.semaphore_signal(
+            barrier, inc=1, device_id_type=MESH,
+            device_id=dev(x, y, k // 4, (k // 2) % 2, k % 2))
+    pl.semaphore_wait(barrier, 30)
+
+    to_partner = rdma(p_ref.at[1 - c], cbuf, cs, cr, partner)
+    to_partner.start()
+    to_partner.wait()
+    q = p_ref[c] + cbuf[...]
+    qb[...] = q.astype(jnp.bfloat16)
+    qf[...] = p_ref[c, t_me] + cbuf[t_me]
+
+    order = sorted(range(1, 16), key=lambda d: -(min(d // 4, 4 - d // 4) + min(d % 4, 4 - d % 4)))
+    sends = []
+    for d in order:
+        tx, ty = (x + d // 4) % NX, (y + d % 4) % NY
+        cp = rdma(qb.at[tx * NY + ty], xbuf.at[d], xs.at[d], xr.at[d], dev(tx, ty, zh, zl, c))
+        cp.start()
+        sends.append(cp)
+    total = qf[...]
+    for d, cp in zip(order, sends):
+        cp.wait_recv()
+        total = total + xbuf[d].astype(jnp.float32)
+    for k in range(4):
+        zsend[k] = total[OWN * k : OWN * (k + 1)]
+    for cp in sends:
+        cp.wait_send()
+
+    own_z = zl == c
+    zcopies = []
+    for dh in range(4):
+        for c2 in range(2):
+            th = (zh + dh) % NZH
+            slab = (th % 2) * 2 + c2
+            slot = dh * 2 + zl
+            j = dh * 2 + c2
+            cp = rdma(zsend.at[slab], zbuf.at[slot], zs.at[j], zr.at[slot], dev(x, y, th, c, c2))
+            if dh == 0:
+                here = own_z & (c == c2)
+
+                @pl.when(here)
+                def _():
+                    zbuf[slot] = zsend[slab]
+
+                @pl.when(jnp.logical_not(here))
+                def _():
+                    cp.start()
+            else:
+                here = None
+                cp.start()
+            zcopies.append((cp, here))
+    for slot in range(8):
+        cp = rdma(zsend.at[0], zbuf.at[slot], zs.at[0], zr.at[slot], partner)
+        if slot < 2:
+            @pl.when(jnp.logical_not(own_z & (zl == slot)))
+            def _():
+                cp.wait_recv()
+        else:
+            cp.wait_recv()
+    acc = zbuf[0]
+    for slot in range(1, 8):
+        acc = acc + zbuf[slot]
+    for cp, here in zcopies:
+        if here is None:
+            cp.wait_send()
+        else:
+            @pl.when(jnp.logical_not(here))
+            def _():
+                cp.wait_send()
+    grad = jnp.where(zh >= 2, acc[:, 64:], acc[:, :64]) / N_DEV
+
+    updated, first_new, second_new = adam_update(grad, par_ref[...], m_ref[...], v_ref[...])
+    first_ref[...] = first_new
+    second_ref[...] = second_new
+    ubuf[...] = updated
+
+    k_me = zh * 2 + c
+    ucopies = []
+    for dh in range(4):
+        for l2 in range(2):
+            th = (zh + dh) % NZH
+            j = dh * 2 + l2
+            cp = rdma(ubuf, abuf.at[k_me], us.at[j], ur.at[k_me], dev(x, y, th, l2, zl))
+            if dh == 0:
+                here = own_z & (zl == l2)
+
+                @pl.when(here)
+                def _():
+                    abuf[k_me] = ubuf[...]
+
+                @pl.when(jnp.logical_not(here))
+                def _():
+                    cp.start()
+            else:
+                here = None
+                cp.start()
+            ucopies.append((cp, here))
+    for k in range(8):
+        cp = rdma(ubuf, abuf.at[k], us.at[0], ur.at[k], partner)
+
+        @pl.when(jnp.logical_not(own_z & (k_me == k)))
+        def _():
+            cp.wait_recv()
+
+        rows[OWN * k : OWN * (k + 1), :] = abuf[k].astype(jnp.float32)
+    for cp, here in ucopies:
+        if here is None:
+            cp.wait_send()
+        else:
+            @pl.when(jnp.logical_not(here))
+            def _():
+                cp.wait_send()
+    gbuf[c, t_me] = jnp.concatenate([rows[:HALF], rows[HALF:]], axis=1).astype(jnp.bfloat16)
+
+    sends = []
+    for d in order:
+        tx, ty = (x + d // 4) % NX, (y + d % 4) % NY
+        cp = rdma(gbuf.at[c, t_me], gbuf.at[c, t_me], bs.at[d], br.at[d], dev(tx, ty, zh, zl, c))
+        cp.start()
+        sends.append(cp)
+    forwards = []
+    cp = rdma(gbuf.at[c, t_me], gbuf.at[c, t_me], fs.at[0], fr.at[0], partner)
+    cp.start()
+    forwards.append(cp)
+    for d in sorted(order, key=lambda d: (min(d // 4, 4 - d // 4) + min(d % 4, 4 - d % 4))):
+        src = ((x + NX - d // 4) % NX) * NY + (y + NY - d % 4) % NY
+        arrived = rdma(gbuf.at[c, src], gbuf.at[c, src], bs.at[d], br.at[d], partner)
+        arrived.wait_recv()
+        cp = rdma(gbuf.at[c, src], gbuf.at[c, src], fs.at[d], fr.at[d], partner)
+        cp.start()
+        forwards.append(cp)
+    for cp in sends:
+        cp.wait_send()
+    for cp in forwards:
+        cp.wait_send()
+    for d in range(16):
+        src = ((x + NX - d // 4) % NX) * NY + (y + NY - d % 4) % NY
+        rdma(gbuf.at[1 - c, src], gbuf.at[1 - c, src], fs.at[d], fr.at[d], partner).wait_recv()
+    g_ref[...] = gbuf[...]
+
+
+def exchange(packed, params, first, second):
+    vm = pl.BlockSpec(memory_space=pltpu.VMEM)
+    dma = pltpu.SemaphoreType.DMA
+    return pl.pallas_call(
+        exchange_kernel,
+        out_shape=(
+            jax.ShapeDtypeStruct(first.shape, jnp.float32),
+            jax.ShapeDtypeStruct(second.shape, jnp.float32),
+            jax.ShapeDtypeStruct((2, 16, HALF, 128), jnp.bfloat16),
+        ),
+        in_specs=[vm] * 4,
+        out_specs=(vm,) * 3,
+        scratch_shapes=[
+            pltpu.VMEM((16, HALF, 128), jnp.float32),
+            pltpu.VMEM((HALF, 128), jnp.float32),
+            pltpu.VMEM((16, HALF, 128), jnp.bfloat16),
+            pltpu.VMEM((16, HALF, 128), jnp.bfloat16),
+            pltpu.VMEM((4, OWN, 128), jnp.float32),
+            pltpu.VMEM((8, OWN, 128), jnp.float32),
+            pltpu.VMEM((OWN, 64), jnp.bfloat16),
+            pltpu.VMEM((8, OWN, 64), jnp.bfloat16),
+            pltpu.VMEM((2 * HALF, 64), jnp.float32),
+            pltpu.VMEM((2, 16, HALF, 128), jnp.bfloat16),
+            dma, dma,
+            dma((16,)), dma((16,)),
+            dma((8,)), dma((8,)),
+            dma((8,)), dma((8,)),
+            dma((16,)), dma((16,)),
+            dma((16,)), dma((16,)),
+        ],
+        compiler_params=pltpu.CompilerParams(collective_id=0, has_side_effects=True),
+        name="exchange",
+    )(packed, params, first, second)
 
 
 def on_device(
@@ -59,10 +274,9 @@
     second_moment,
 ):
     model_width = hidden_in.shape[1]
-    adapter_rank_size = down_projection_matrix.shape[1]
+    rank = down_projection_matrix.shape[1]
     row_count_total = model_width + up_projection_matrix.shape[1]
-    accelerator_list = lax.axis_size("group") * lax.axis_size("replica")
-    own_rows = row_count_total // accelerator_list
+    own_rows = first_moment.shape[0]
     grad_pre, backward_reduced, scaled_reduced = queries_backward(
         hidden_in,
         query_cotangent,
@@ -71,33 +285,22 @@
         down_projection_matrix,
         up_projection_matrix,
     )
-    stacked = jnp.concatenate([hidden_in, grad_pre], axis=1)
-    operand = jnp.concatenate([backward_reduced, scaled_reduced], axis=1)
-    matrix_product = lax.dot_general(
-        stacked, operand, (((0,), (0,)), ((), ())), preferred_element_type=jnp.float32
-    )
-    row_ids = lax.iota(jnp.int32, lax.axis_size(("group", "replica")) * own_rows)
-    is_down_matrix = (row_ids < model_width)[:, None]
-    grad_own = lax.psum_scatter(
-        jnp.where(
-            is_down_matrix,
-            matrix_product[:, :adapter_rank_size],
-            matrix_product[:, adapter_rank_size:],
-        )
-        / accelerator_list,
-        ("group", "replica"),
-        scatter_dimension=0,
-        tiled=True,
-    )
+    over_tokens = (((0,), (0,)), ((), ()))
+    down_term = lax.dot_general(
+        hidden_in, backward_reduced, over_tokens, preferred_element_type=jnp.float32)
+    up_term = lax.dot_general(
+        grad_pre, scaled_reduced, over_tokens, preferred_element_type=jnp.float32)
+    term = jnp.concatenate([down_term, up_term], axis=0)
+    packed = term.reshape(NX, 2, NY, 2, HALF, rank).transpose(1, 0, 2, 4, 3, 5)
+    packed = packed.reshape(2, NX * NY, HALF, 2 * rank)
     owner = lax.axis_index(("group", "replica"))
     combined = jnp.concatenate([down_projection_matrix, up_projection_matrix.T], axis=0)
     params_own = lax.dynamic_slice_in_dim(combined, owner * own_rows, own_rows, 0).astype(
         jnp.float32
     )
-    updated_own, first_new, second_new = adam_update(
-        grad_own, params_own, first_moment, second_moment
-    )
-    gathered = lax.all_gather(updated_own, ("group", "replica"), axis=0, tiled=True)
+    first_new, second_new, gathered = exchange(packed, params_own, first_moment, second_moment)
+    gathered = gathered.reshape(2, NX, NY, HALF, 2, rank).transpose(1, 0, 2, 4, 3, 5)
+    gathered = gathered.reshape(row_count_total, rank)
     return (gathered[:model_width], gathered[model_width:].T, first_new, second_new)
 
 

time: 661 us -> 107 us (0.16)
  blocking collectives: 349 us -> 0 us
  waiting for transfers between devices: 262 us -> 0 us
  Pallas kernels: 0 us -> 38.6 us
  local copies, waits for them, and re-layouts: 16.3 us -> 43.8 us
  between operations: 14.2 us -> 0.77 us
    all_gather x1 -> x0, blocking collectives: 349 us -> none  [on_device(): lax.all_gather(updated_own, ('group', 'replica'), axis=0, tiled=True)]
    unnamed x2 -> x0, waiting for transfers between devices: 262 us -> none
    pallas_call x0 -> x1, Pallas kernels: none -> 38.6 us  [exchange(): pl.pallas_call(exchange_kernel, out_shape=(jax.ShapeDtypeStruct(first.sha...]
    reshape x0 -> x5, local copies, waits for them, and re-layouts: none -> 21.7 us  [the longest x2 11.6 us: on_device(): packed = term.reshape(NX, 2, NY, 2, HALF, rank).transpose(1, 0, 2, 4, 3, 5)]
  transfers between devices with their start and end apart: 1 -> 0, of which waited for: 1 -> 0; matrix products, arithmetic and copies ran while one was open for 0% -> 0% of each run, Pallas kernels for 0% -> 0%
where the time goes in v1:
time: 107 us; the launch traced here: 106 us
  local copies, waits for them, and re-layouts  43.8 us (41%)
  Pallas kernels  38.6 us (36%)
  matrix products  12.4 us (12%)
  other arithmetic  10.5 us (10%)
    pallas_call x1, Pallas kernels, exchange(): pl.pallas_call(exchange_kernel, out_shape=(jax.ShapeDtypeStruct(first.sha...  38.6 us
    reshape x2, local copies, waits for them, and re-layouts, on_device(): packed = term.reshape(NX, 2, NY, 2, HALF, rank).transpose(1, 0, 2, 4, 3, 5)  11.6 us
    dot_general x1, matrix products, queries_backward(): jnp.dot(rows_in, w_query, preferred_element_type=jnp.float32)  5.78 us
    mul x2, local copies, waits for them, and re-layouts, queries_backward(): inverse * (upstream - normed * jnp.mean(upstream * normed, axis=-1, keepd...  4.54 us
    mul x2, local copies, waits for them, and re-layouts, queries_backward(): normed * jnp.mean(upstream * normed, axis=-1, keepdims=True)  4.51 us
    reshape x1, local copies, waits for them, and re-layouts, on_device(): gathered = gathered.reshape(row_count_total, rank)  3.9 us
    convert_element_type x1, other arithmetic, queries_backward(): grad_pre = grad_pre.reshape(token_count, -1).astype(jnp.bfloat16)  3.7 us
    reshape x1, local copies, waits for them, and re-layouts, on_device(): packed = packed.reshape(2, NX * NY, HALF, 2 * rank)  3.56 us

profile of v1, /device:TPU:1, one launch (start us, length us, event | category | flops | bytes accessed | tf_op | source)
XLA Modules:
  0.0 106.1 jit_solution(6267804868176510658)
XLA Ops:
  0.6 0.0 copy-start
  0.6 1.5 %copy-done = bf16[320,3072]{1,0:T(8,128)(2,1)S(1)} copy-done((bf16[320,3072]{1,0:T(8,128)(2,1)S(1)}, bf16[320,3072]{1,0:T(8,128)(2,1)}, u32[]{:S(2)}) %copy-start) | copy-done | bytes 1966104
  2.2 1.7 %convolution_convert_fusion = bf16[320,64]{0,1:T(8,128)(2,1)S(1)} fusion(bf16[320,3072]{1,0:T(8,128)(2,1)S(1)} %copy-done, bf16[3072,64]{0,1:T(8,128)(2,1)} %param.11), kind=kOutput, calls=%fused_computation.11 | convolution fusion | flops 125849600 | bytes 2400256 | tf_op jit(solution)/shard_map/dot_general | solution.py:29
  3.9 0.0 copy-start.2
  3.9 5.8 %fusion.9 = f32[320,1536]{1,0:T(8,128)S(1)} fusion(bf16[320,3072]{1,0:T(8,128)(2,1)S(1)} %copy-done, bf16[3072,1536]{1,0:T(8,128)(2,1)} %param.9), kind=kOutput, calls=%fused_computation.24 | convolution fusion | flops 3019898880 | bytes 13369344 | tf_op jit(solution)/shard_map/dot_general | solution.py:32
  9.7 0.0 copy-done.2
  9.7 1.7 %fusion = f32[320,1536]{1,0:T(8,128)} fusion(f32[320,1536]{1,0:T(8,128)S(1)} %fusion.9, bf16[320,64]{0,1:T(8,128)(2,1)S(1)} %convolution_convert_fusion, bf16[64,1536]{1,0:T(8,128)(2,1)S(1)} %copy-done.2), kind=kOutput, calls=%fused_computation.2 | convolution fusion | flops 63897600 | bytes 4169728 | tf_op jit(solution)/shard_map/dot_general | solution.py:33
  11.5 3.0 %copy.24 = f32[320,1536]{0,1:T(8,128)} copy(f32[320,1536]{1,0:T(8,128)} %fusion) | data formatting | bytes 3932160 | tf_op jit(solution)/shard_map/add | solution.py:33
  14.4 0.0 copy-start.1
  14.4 2.0 %multiply_reduce_fusion.1 = f32[320,12]{0,1:T(8,128)S(1)} fusion(f32[320,12,128]{0,2,1:T(8,128)} %bitcast.29), kind=kLoop, calls=%fused_computation.4 | loop fusion | flops 979200 | bytes 1981440 | tf_op jit(solution)/shard_map/reduce_sum | solution.py:39
  16.4 0.0 copy-start.6
  16.4 0.0 copy-done.1
  16.5 1.8 %copy.26 = f32[320,1536]{0,1:T(8,128)} copy(bf16[320,1536]{1,0:T(8,128)(2,1)S(1)} %copy-done.1) | data formatting | bytes 2949120 | tf_op jit(solution)/shard_map/convert_element_type | solution.py:41
  18.2 0.0 copy-done.6
  18.2 2.9 %multiply_reduce_fusion = f32[320,12]{0,1:T(8,128)S(1)} fusion(f32[320,12,128]{0,2,1:T(8,128)} %bitcast.30, f32[320,12,128]{0,2,1:T(8,128)} %bitcast.31, f32[128]{0:T(128)S(1)} %copy-done.6, f32[320,12]{0,1:T(8,128)S(1)} %add_rsqrt_fusion), kind=kLoop, calls=%fused_computation.3 | loop fusion | flops 1962240 | bytes 3963392 | tf_op jit(solution)/shard_map/reduce_sum | solution.py:42
  21.1 1.5 %mul.86 = f32[320,12,128]{0,2,1:T(8,128)} broadcast(f32[320,12]{0,1:T(8,128)S(1)} %broadcast_multiply_fusion), dimensions={0,1} | broadcast | bytes 1981440 | tf_op jit(solution)/shard_map/mul | solution.py:42
  22.7 3.0 %copy.27 = f32[320,1536]{1,0:T(8,128)} copy(f32[320,1536]{0,1:T(8,128)} %bitcast.32) | data formatting | bytes 3932160 | tf_op jit(solution)/shard_map/mul | solution.py:42
  25.6 1.6 %mul.75 = f32[320,12,128]{0,2,1:T(8,128)} broadcast(f32[320,12]{0,1:T(8,128)S(1)} %add_rsqrt_fusion), dimensions={0,1} | broadcast | bytes 1981440 | tf_op jit(solution)/shard_map/mul | solution.py:42
  27.2 3.0 %copy.28 = f32[320,1536]{1,0:T(8,128)} copy(f32[320,1536]{0,1:T(8,128)} %bitcast.33) | data formatting | bytes 3932160 | tf_op jit(solution)/shard_map/mul | solution.py:42
  30.2 3.7 %multiply_convert_fusion = bf16[320,1536]{1,0:T(8,128)(2,1)S(1)} fusion(f32[320,1536]{1,0:T(8,128)} %copy.28, f32[320,1536]{1,0:T(8,128)} %copy.27, f32[320,1536]{1,0:T(8,128)} %fusion, f32[1536]{0:T(1024)S(1)} %broadcast_bitcast_fusion, bf16[320,1536]{1,0:T(8,128)(2,1)} %param.13), kind=kLoop, calls=%fused_computation.5 | loop fusion | flops 3440640 | bytes 7870464 | tf_op jit(solution)/shard_map/convert_element_type | solution.py:43
  33.9 1.1 fusion.2
  34.9 2.1 %convolution_bitcast_fusion = f32[3072,64]{0,1:T(8,128)} fusion(bf16[320,3072]{1,0:T(8,128)(2,1)S(1)} %copy-done, bf16[320,1536]{1,0:T(8,128)(2,1)S(1)} %multiply_convert_fusion, bf16[64,1536]{1,0:T(8,128)(2,1)S(1)} %copy-done.2), kind=kOutput, calls=%fused_computation | convolution fusion | flops 188784640 | bytes 3932160 | tf_op jit(solution)/shard_map/dot_general | solution.py:289
  37.0 1.3 %pad_maximum_fusion = f32[4608,64]{0,1:T(8,128)S(1)} fusion(f32[1536,64]{0,1:T(8,128)} %fusion.2, f32[3072,64]{0,1:T(8,128)} %convolution_bitcast_fusion), kind=kLoop, calls=%fused_computation.6 | loop fusion | flops 294912 | bytes 2359296 | tf_op jit(solution)/shard_map/concatenate | solution.py:293
  38.3 5.5 %reshape.46 = f32[4,2,4,2,72,64]{4,3,2,1,0,5:T(2,128)} reshape(f32[4608,64]{0,1:T(8,128)S(1)} %pad_maximum_fusion) | data formatting | bytes 2359296 | tf_op jit(solution)/shard_map/reshape | solution.py:294
  43.8 6.2 %copy.29 = f32[4,2,4,2,72,64]{5,3,4,2,0,1:T(2,128)} copy(f32[4,2,4,2,72,64]{4,3,2,1,0,5:T(2,128)} %reshape.46) | data formatting | bytes 2359296 | tf_op jit(solution)/shard_map/reshape | solution.py:294
  50.0 0.0 copy-start.3
  50.0 3.6 %reshape.47.p_ref = f32[2,16,72,128]{3,2,1,0:T(8,128)} reshape(f32[2,4,4,72,2,64]{5,4,3,2,1,0:T(2,128)} %bitcast.34) | data formatting | bytes 2359296 | tf_op jit(solution)/shard_map/reshape | solution.py:295
  53.5 0.0 copy-done.3
  53.5 0.4 copy.31
  53.9 0.2 copy.30
  54.2 0.6 fusion.6.par_ref
  54.8 38.6 %exchange.1 = (f32[18,64]{1,0:T(8,128)}, f32[18,64]{1,0:T(8,128)}, bf16[2,16,72,128]{3,2,1,0:T(8,128)(2,1)}) custom-call(f32[2,16,72,128]{3,2,1,0:T(8,128)} %reshape.47.p_ref, f32[18,64]{1,0:T(8,128)} %fusion.6.par_ref, f32[18,64]{1,0:T(8,128)} %m_ref.1, f32[18,64]{1,0:T(8,128)} %v_ref.1), custom_call_target="tpu_custom_call" | custom-call | tf_op jit(solution)/shard_map/exchange/pallas_call | solution.py:234
  93.4 2.6 %reshape.48 = bf16[2,4,4,72,2,64]{5,4,3,2,1,0:T(2,128)(2,1)S(1)} reshape(bf16[2,16,72,128]{3,2,1,0:T(8,128)(2,1)} %get-tuple-element.7) | data formatting | bytes 1179648 | tf_op jit(solution)/shard_map/reshape | solution.py:302
  96.1 3.4 %copy.32 = bf16[4,2,4,2,72,64]{4,3,2,1,0,5:T(2,128)(2,1)} copy(bf16[4,2,4,2,72,64]{5,3,4,2,0,1:T(2,128)(2,1)S(1)} %bitcast.35) | data formatting | bytes 1179648 | tf_op jit(solution)/shard_map/transpose | solution.py:302
  99.5 0.0 copy-start.5
  99.5 0.0 copy-start.4
  99.5 3.9 %reshape.49 = bf16[4608,64]{0,1:T(8,128)(2,1)S(1)} reshape(bf16[4,2,4,2,72,64]{4,3,2,1,0,5:T(2,128)(2,1)} %copy.32) | data formatting | bytes 1179648 | tf_op jit(solution)/shard_map/reshape | solution.py:303
  103.4 0.8 slice.8
  104.2 0.7 slice_bitcast_fusion
  104.9 0.0 copy-done.5
  104.9 0.6 copy.35
  105.5 0.0 copy-done.4
  105.5 0.6 copy.36
  (3 shorter events, 0.0 us)
Async XLA Ops:
  0.6 1.6 %copy-start = (bf16[320,3072]{1,0:T(8,128)(2,1)S(1)}, bf16[320,3072]{1,0:T(8,128)(2,1)}, u32[]{:S(2)}) copy-start(bf16[320,3072]{1,0:T(8,128)(2,1)} %param.8) | copy-start | bytes 5898244
  3.9 5.8 %copy-start.2 = (bf16[64,1536]{1,0:T(8,128)(2,1)S(1)}, bf16[64,1536]{1,0:T(8,128)(2,1)}, u32[]{:S(2)}) copy-start(bf16[64,1536]{1,0:T(8,128)(2,1)} %param.12) | copy-start | bytes 589828
  14.4 2.0 %copy-start.1 = (bf16[320,1536]{1,0:T(8,128)(2,1)S(1)}, bf16[320,1536]{1,0:T(8,128)(2,1)}, u32[]{:S(2)}) copy-start(bf16[320,1536]{1,0:T(8,128)(2,1)} %param.13) | copy-start | bytes 2949124
  16.4 1.8 %copy-start.6 = (f32[128]{0:T(128)S(1)}, f32[128]{0:T(128)}, u32[]{:S(2)}) copy-start(f32[128]{0:T(128)} %param.10) | copy-start | bytes 1540
  50.0 3.6 %copy-start.3 = (bf16[3072,64]{0,1:T(8,128)(2,1)S(1)}, bf16[3072,64]{0,1:T(8,128)(2,1)}, u32[]{:S(2)}) copy-start(bf16[3072,64]{0,1:T(8,128)(2,1)} %param.11) | copy-start | bytes 1179652
  99.5 5.4 %copy-start.5 = (f32[18,64]{1,0:T(8,128)S(1)}, f32[18,64]{1,0:T(8,128)}, u32[]{:S(2)}) copy-start(f32[18,64]{1,0:T(8,128)} %get-tuple-element.16) | copy-start | bytes 13828
  99.5 6.0 %copy-start.4 = (f32[18,64]{1,0:T(8,128)S(1)}, f32[18,64]{1,0:T(8,128)}, u32[]{:S(2)}) copy-start(f32[18,64]{1,0:T(8,128)} %get-tuple-element.17) | copy-start | bytes 13828

commit v2 on v1

v2 whole, which is shorter than its diff:
```python
import jax
import jax.numpy as jnp
from jax import lax
from jax.experimental import pallas as pl
from jax.experimental.pallas import tpu as pltpu
from jax.sharding import PartitionSpec as P

adapter_scale_factor = 0.5
norm_epsilon = 1e-06
beta_one = 0.9
beta_two = 0.999
first_bias = 1.0 - 0.9**10
second_bias = 1.0 - 0.999**10
learn_rate = 0.001
adam_eps = 1e-08

MESH = pl.DeviceIdType.MESH
NX, NY, NZH = 4, 4, 4
OWN = 18
HALF = 72
N_DEV = 256
TOK, D, QW, R, HD = 320, 3072, 1536, 64, 128
ROWS = D + QW
WC = 256
NW = QW // WC
XROWS = ROWS // NX
RB = 64

F32, BF16 = jnp.float32, jnp.bfloat16


def adam_update(grads, params, first, second):
    first_new = beta_one * first + (1.0 - beta_one) * grads
    second_new = beta_two * second + (1.0 - beta_two) * grads * grads
    direction = first_new / first_bias / (jnp.sqrt(second_new / second_bias) + adam_eps)
    return ((params - learn_rate * direction).astype(jnp.bfloat16), first_new, second_new)


def hops(d):
    return min(d // 4, 4 - d // 4) + min(d % 4, 4 - d % 4)


def contract(a, b, da, db):
    return lax.dot_general(a, b, (((da,), (db,)), ((), ())), preferred_element_type=F32)


def step_kernel(
    hid_hbm, w_hbm, gain_hbm, dnt_hbm, up_hbm, cot_hbm, m_hbm, v_hbm,
    first_ref, second_ref, g_ref,
    stacked, wbuf, gain, dnt, up, cot, m_ref, v_ref,
    proj, slow, slowt, blt, gt, grows,
    psend, cbuf, qf, qb, xbuf, zsend, zbuf, ubuf, abuf, rows, gbuf,
    ls, ws, cs, cr, xs, xr, zs, zr, us, ur, bs, br, fs, fr,
):
    g = lax.axis_index("group")
    r = lax.axis_index("replica")
    x, zl = g // 2, g % 2
    y, zh, c = r // 8, (r // 2) % 4, r % 2
    t_me = x * NY + y

    def dev(x_, y_, zh_, zl_, c_):
        return (x_ * 2 + zl_, y_ * 8 + zh_ * 2 + c_)

    def rdma(src, dst, ssem, rsem, to):
        return pltpu.make_async_remote_copy(
            src_ref=src, dst_ref=dst, send_sem=ssem, recv_sem=rsem,
            device_id=to, device_id_type=MESH)

    partner = dev(x, y, zh, zl, 1 - c)

    loads = [
        pltpu.make_async_copy(src, dst, ls.at[i])
        for i, (src, dst) in enumerate([
            (hid_hbm, stacked.at[:, :D]), (dnt_hbm, dnt), (up_hbm, up), (cot_hbm, cot),
            (gain_hbm, gain), (m_hbm, m_ref), (v_hbm, v_ref)])
    ]
    wloads = [
        pltpu.make_async_copy(w_hbm.at[:, WC * k : WC * (k + 1)], wbuf.at[k], ws.at[k])
        for k in range(NW)
    ]
    loads[0].start()
    loads[1].start()
    wloads[0].start()
    loads[2].start()
    loads[4].start()
    wloads[1].start()
    loads[3].start()
    for k in range(2, NW):
        wloads[k].start()
    loads[5].start()
    loads[6].start()

    barrier = pltpu.get_barrier_semaphore()
    for d in range(1, 16):
        pl.semaphore_signal(
            barrier, inc=1, device_id_type=MESH,
            device_id=dev((x + d // 4) % NX, (y + d % 4) % NY, zh, zl, c))
    for d in range(1, 16):
        k = (zh * 4 + zl * 2 + c + d) % 16
        pl.semaphore_signal(
            barrier, inc=1, device_id_type=MESH,
            device_id=dev(x, y, k // 4, (k // 2) % 2, k % 2))

    loads[0].wait()
    loads[1].wait()
    low = contract(stacked[:, :D], dnt[...], 1, 1).astype(BF16).astype(F32) * adapter_scale_factor
    slow[...] = low.astype(BF16)
    slowt[...] = low.T.astype(BF16)
    loads[2].wait()
    loads[4].wait()

    def to_rows(j):
        grows[HD * j : HD * (j + 1), :] = gt[:, HD * j : HD * (j + 1)].T

    def backward(k):
        if k == 0:
            loads[3].wait()
        for h in range(2):
            lanes = slice(WC * k + HD * h, WC * k + HD * (h + 1))
            for b in range(TOK // RB):
                tok = slice(RB * b, RB * (b + 1))
                p = proj[k % 2, tok, HD * h : HD * (h + 1)]
                inverse = lax.rsqrt(jnp.mean(p * p, axis=-1, keepdims=True) + norm_epsilon)
                normed = p * inverse
                upstream = cot[tok, lanes].astype(F32) * gain[...]
                along = jnp.mean(upstream * normed, axis=-1, keepdims=True)
                stacked[tok, D + lanes.start : D + lanes.stop] = (
                    inverse * (upstream - normed * along)).astype(BF16)
        lanes = slice(D + WC * k, D + WC * (k + 1))
        gp = stacked[:, lanes]
        back = contract(up[:, WC * k : WC * (k + 1)], gp, 1, 1)
        if k == 0:
            blt[...] = back
        else:
            blt[...] += back
        gt[:, lanes] = jnp.dot(slowt[...], gp, preferred_element_type=F32)
        for j in range(lanes.start // HD, lanes.stop // HD):
            to_rows(j)

    for k in range(NW):
        wloads[k].wait()
        proj[k % 2] = jnp.dot(stacked[:, :D], wbuf[k], preferred_element_type=F32) + jnp.dot(
            slow[...], up[:, WC * k : WC * (k + 1)], preferred_element_type=F32)
        if k:
            backward(k - 1)
    backward(NW - 1)
    back = (adapter_scale_factor * blt[...]).astype(BF16)
    for j in range(D // WC):
        lanes = slice(WC * j, WC * (j + 1))
        gt[:, lanes] = jnp.dot(back, stacked[:, lanes], preferred_element_type=F32)
        to_rows(2 * j)
        to_rows(2 * j + 1)

    def block(x_, zl_, y_):
        o = pl.multiple_of(x_ * XROWS + zl_ * (XROWS // 2) + y_ * 2 * HALF, 8)
        return jnp.concatenate([grows[pl.ds(o, HALF), :], grows[pl.ds(o + HALF, HALF), :]], axis=1)

    pl.semaphore_wait(barrier, 30)

    dxs = (2, 1, 3, 0)
    pair = []
    for i, dx in enumerate(dxs):
        tx = (x + dx) % NX
        for ty in range(NY):
            psend[i, ty] = block(tx, 1 - c, ty)
        cp = rdma(psend.at[i], cbuf.at[i], cs.at[i], cr.at[i], partner)
        cp.start()
        pair.append(cp)

    sends = []
    for i, dx in enumerate(dxs):
        tx = (x + dx) % NX
        pair[i].wait_recv()
        for ty in range(NY):
            qb[i, ty] = (block(tx, c, ty) + cbuf[i, ty]).astype(BF16)
        if dx == 0:
            qf[...] = block(tx, c, y) + cbuf[i, y]
        for dy in (2, 1, 3, 0):
            d = dx * 4 + dy
            if d:
                ty = (y + dy) % NY
                cp = rdma(qb.at[i, ty], xbuf.at[d], xs.at[d], xr.at[d], dev(tx, ty, zh, zl, c))
                cp.start()
                sends.append((d, cp))

    for i in (5, 6):
        loads[i].wait()
    mine = (g * 32 + r) * OWN + lax.broadcasted_iota(jnp.int32, (OWN, D), 0)
    at = lax.broadcasted_iota(jnp.int32, (OWN, D), 1)
    pick_down = (at == mine).astype(F32).astype(BF16)
    pick_up = (at[:, :QW] + D == mine[:, :QW]).astype(F32).astype(BF16)
    params = contract(pick_down, dnt[...], 1, 1) + contract(pick_up, up[...], 1, 1)

    total = qf[...]
    for d, cp in sends:
        cp.wait_recv()
        total = total + xbuf[d].astype(F32)
    for k in range(4):
        zsend[k] = total[OWN * k : OWN * (k + 1)]
    for d, cp in sends:
        cp.wait_send()
    for cp in pair:
        cp.wait_send()

    own_z = zl == c
    zcopies = []
    for dh in range(4):
        for c2 in range(2):
            th = (zh + dh) % NZH
            slab = (th % 2) * 2 + c2
            slot = dh * 2 + zl
            j = dh * 2 + c2
            cp = rdma(zsend.at[slab], zbuf.at[slot], zs.at[j], zr.at[slot], dev(x, y, th, c, c2))
            if dh == 0:
                here = own_z & (c == c2)

                @pl.when(here)
                def _():
                    zbuf[slot] = zsend[slab]

                @pl.when(jnp.logical_not(here))
                def _():
                    cp.start()
            else:
                here = None
                cp.start()
            zcopies.append((cp, here))
    for slot in range(8):
        cp = rdma(zsend.at[0], zbuf.at[slot], zs.at[0], zr.at[slot], partner)
        if slot < 2:
            @pl.when(jnp.logical_not(own_z & (zl == slot)))
            def _():
                cp.wait_recv()
        else:
            cp.wait_recv()
    acc = zbuf[0]
    for slot in range(1, 8):
        acc = acc + zbuf[slot]
    for cp, here in zcopies:
        if here is None:
            cp.wait_send()
        else:
            @pl.when(jnp.logical_not(here))
            def _():
                cp.wait_send()
    grad = jnp.where(zh >= 2, acc[:, 64:], acc[:, :64]) / N_DEV

    updated, first_new, second_new = adam_update(grad, params, m_ref[...], v_ref[...])
    first_ref[...] = first_new
    second_ref[...] = second_new
    ubuf[...] = updated

    k_me = zh * 2 + c
    ucopies = []
    for dh in range(4):
        for l2 in range(2):
            th = (zh + dh) % NZH
            j = dh * 2 + l2
            cp = rdma(ubuf, abuf.at[k_me], us.at[j], ur.at[k_me], dev(x, y, th, l2, zl))
            if dh == 0:
                here = own_z & (zl == l2)

                @pl.when(here)
                def _():
                    abuf[k_me] = ubuf[...]

                @pl.when(jnp.logical_not(here))
                def _():
                    cp.start()
            else:
                here = None
                cp.start()
            ucopies.append((cp, here))
    for k in range(8):
        cp = rdma(ubuf, abuf.at[k], us.at[0], ur.at[k], partner)

        @pl.when(jnp.logical_not(own_z & (k_me == k)))
        def _():
            cp.wait_recv()

        rows[OWN * k : OWN * (k + 1), :] = abuf[k].astype(jnp.float32)
    for cp, here in ucopies:
        if here is None:
            cp.wait_send()
        else:
            @pl.when(jnp.logical_not(here))
            def _():
                cp.wait_send()
    gbuf[c, t_me] = jnp.concatenate([rows[:HALF], rows[HALF:]], axis=1).astype(jnp.bfloat16)

    sends = []
    order = sorted(range(1, 16), key=hops)
    for d in order[::-1]:
        tx, ty = (x + d // 4) % NX, (y + d % 4) % NY
        cp = rdma(gbuf.at[c, t_me], gbuf.at[c, t_me], bs.at[d], br.at[d], dev(tx, ty, zh, zl, c))
        cp.start()
        sends.append(cp)
    forwards = []
    cp = rdma(gbuf.at[c, t_me], gbuf.at[c, t_me], fs.at[0], fr.at[0], partner)
    cp.start()
    forwards.append(cp)
    for d in order:
        src = ((x + NX - d // 4) % NX) * NY + (y + NY - d % 4) % NY
        arrived = rdma(gbuf.at[c, src], gbuf.at[c, src], bs.at[d], br.at[d], partner)
        arrived.wait_recv()
        cp = rdma(gbuf.at[c, src], gbuf.at[c, src], fs.at[d], fr.at[d], partner)
        cp.start()
        forwards.append(cp)
    for cp in sends:
        cp.wait_send()
    for cp in forwards:
        cp.wait_send()
    for d in range(16):
        src = ((x + NX - d // 4) % NX) * NY + (y + NY - d % 4) % NY
        rdma(gbuf.at[1 - c, src], gbuf.at[1 - c, src], fs.at[d], fr.at[d], partner).wait_recv()
    g_ref[...] = gbuf[...]


def unpack_kernel(g_ref, first_in, second_in, down_ref, up_ref, first_ref, second_ref, full):
    for x in range(NX):
        for zl in range(2):
            for y in range(NY):
                o = (x * 8 + zl * 4 + y) * 2 * HALF
                blk = g_ref[zl, x * NY + y].astype(F32)
                full[o : o + HALF, :] = blk[:, :R]
                full[o + HALF : o + 2 * HALF, :] = blk[:, R:]
    for j in range(ROWS // HD):
        tile = full[HD * j : HD * (j + 1), :].T.astype(BF16)
        if j < D // HD:
            down_ref[:, HD * j : HD * (j + 1)] = tile
        else:
            up_ref[:, HD * j - D : HD * (j + 1) - D] = tile
    first_ref[...] = first_in[...]
    second_ref[...] = second_in[...]


def on_device(
    hidden_in,
    w_query,
    query_gain,
    down_projection_matrix,
    up_projection_matrix,
    query_cotangent,
    first_moment,
    second_moment,
):
    vm = pl.BlockSpec(memory_space=pltpu.VMEM)
    anywhere = pl.BlockSpec(memory_space=pl.ANY)
    dma = pltpu.SemaphoreType.DMA
    own = jax.ShapeDtypeStruct((OWN, R), F32)
    first, second, gathered = pl.pallas_call(
        step_kernel,
        out_shape=(own, own, jax.ShapeDtypeStruct((2, 16, HALF, 128), BF16)),
        in_specs=[anywhere] * 8,
        out_specs=(vm,) * 3,
        scratch_shapes=[
            pltpu.VMEM((TOK, ROWS), BF16),
            pltpu.VMEM((NW, D, WC), BF16),
            pltpu.VMEM((1, HD), F32),
            pltpu.VMEM((R, D), BF16),
            pltpu.VMEM((R, QW), BF16),
            pltpu.VMEM((TOK, QW), BF16),
            pltpu.VMEM((OWN, R), F32),
            pltpu.VMEM((OWN, R), F32),
            pltpu.VMEM((2, TOK, WC), F32),
            pltpu.VMEM((TOK, R), BF16),
            pltpu.VMEM((R, TOK), BF16),
            pltpu.VMEM((R, TOK), F32),
            pltpu.VMEM((R, ROWS), F32),
            pltpu.VMEM((ROWS, R), F32),
            pltpu.VMEM((4, 4, HALF, 128), F32),
            pltpu.VMEM((4, 4, HALF, 128), F32),
            pltpu.VMEM((HALF, 128), F32),
            pltpu.VMEM((4, 4, HALF, 128), BF16),
            pltpu.VMEM((16, HALF, 128), BF16),
            pltpu.VMEM((4, OWN, 128), F32),
            pltpu.VMEM((8, OWN, 128), F32),
            pltpu.VMEM((OWN, R), BF16),
            pltpu.VMEM((8, OWN, R), BF16),
            pltpu.VMEM((2 * HALF, R), F32),
            pltpu.VMEM((2, 16, HALF, 128), BF16),
            dma((7,)), dma((NW,)),
            dma((4,)), dma((4,)),
            dma((16,)), dma((16,)),
            dma((8,)), dma((8,)),
            dma((8,)), dma((8,)),
            dma((16,)), dma((16,)),
            dma((16,)), dma((16,)),
        ],
        compiler_params=pltpu.CompilerParams(collective_id=0, has_side_effects=True),
        name="step",
    )(
        hidden_in, w_query, query_gain.reshape(1, HD), down_projection_matrix.T,
        up_projection_matrix, query_cotangent, first_moment, second_moment)
    down, up, first, second = pl.pallas_call(
        unpack_kernel,
        out_shape=(
            jax.ShapeDtypeStruct((R, D), BF16), jax.ShapeDtypeStruct((R, QW), BF16), own, own),
        in_specs=[vm] * 3,
        out_specs=(vm,) * 4,
        scratch_shapes=[pltpu.VMEM((ROWS, R), F32)],
        name="unpack",
    )(gathered, first, second)
    return (down.T, up, first, second)


def solution(mesh):
    placed = (
        P(("group", "replica"), None),
        P(),
        P(),
        P(),
        P(),
        P(("group", "replica"), None),
        P(("group", "replica"), None),
        P(("group", "replica"), None),
    )
    return jax.shard_map(
        on_device,
        mesh=mesh,
        in_specs=placed,
        out_specs=(P(), P(), P(("group", "replica"), None), P(("group", "replica"), None)),
        check_vma=False,
    )
```

time: 107 us -> 48.3 us (0.45)
  local copies, waits for them, and re-layouts: 43.8 us -> 0 us
  matrix products: 12.4 us -> 0 us
  other arithmetic: 10.5 us -> 0 us
  Pallas kernels: 38.6 us -> 47.5 us
    reshape x5 -> x0, local copies, waits for them, and re-layouts: 21.7 us -> none  [the longest x2 11.6 us: on_device(): packed = term.reshape(NX, 2, NY, 2, HALF, rank).transpose(1, 0, 2, 4, 3, 5)]
    dot_general x5 -> x0, matrix products: 12.4 us -> none  [the longest x1 5.78 us: queries_backward(): jnp.dot(rows_in, w_query, preferred_element_type=jnp.float32)]
    mul x5 -> x0, local copies, waits for them, and re-layouts: 9.06 us -> none  [the longest x2 4.54 us: queries_backward(): inverse * (upstream - normed * jnp.mean(upstream * normed, axis=-1, keepd...]
    pallas_call x1 -> x2, Pallas kernels: 38.6 us -> 47.5 us  [the longest x1 45.2 us: on_device(): pl.pallas_call(step_kernel, out_shape=(own, own, jax.ShapeDtypeStruct((2,...]
    reduce_sum x2 -> x0, other arithmetic: 4.83 us -> none  [the longest x1 2.87 us: queries_backward(): jnp.mean(upstream * normed, axis=-1, keepdims=True)]
    convert_element_type x2 -> x0, other arithmetic: 4.35 us -> none  [the longest x1 3.7 us: queries_backward(): grad_pre = grad_pre.reshape(token_count, -1).astype(jnp.bfloat16)]
    transpose x2 -> x0, local copies, waits for them, and re-layouts: 4.12 us -> none  [the longest x1 3.43 us: on_device(): gathered.reshape(2, NX, NY, HALF, 2, rank).transpose(1, 0, 2, 4, 3, 5)]
    unnamed x18 -> x0, local copies, waits for them, and re-layouts: 3.37 us -> none
where the time goes in v2:
time: 48.3 us; the launch traced here: 48.2 us
  Pallas kernels  47.5 us (98%)
  between operations  0.64 us (1%)
    pallas_call x1, Pallas kernels, on_device(): pl.pallas_call(step_kernel, out_shape=(own, own, jax.ShapeDtypeStruct((2,...  45.2 us
    pallas_call x1, Pallas kernels, on_device(): pl.pallas_call(unpack_kernel, out_shape=(jax.ShapeDtypeStruct((R, D), BF1...  2.34 us

profile of v2, /device:TPU:1, one launch (start us, length us, event | category | flops | bytes accessed | tf_op | source)
XLA Modules:
  0.0 48.2 jit_solution(17960815039810752147)
XLA Ops:
  0.6 45.2 %step.1 = (f32[18,64]{1,0:T(8,128)}, f32[18,64]{1,0:T(8,128)}, bf16[2,16,72,128]{3,2,1,0:T(8,128)(2,1)}) custom-call(bf16[320,3072]{1,0:T(8,128)(2,1)} %hid_hbm.1, bf16[3072,1536]{1,0:T(8,128)(2,1)} %w_hbm.1, f32[1,128]{1,0:T(1,128)} %bitcast.4, bf16[64,3072]{1,0:T(8,128)(2,1)} %bitcast.3, bf16[64,1536]{1,0:T(8,128)(2,1)} %up_hbm.1, ...), custom_call_target="tpu_custom_call" | custom-call | tf_op jit(solution)/shard_map/step/pallas_call | solution.py:351
  45.8 2.3 %unpack.1 = (bf16[64,3072]{1,0:T(8,128)(2,1)}, bf16[64,1536]{1,0:T(8,128)(2,1)}, f32[18,64]{1,0:T(8,128)}, f32[18,64]{1,0:T(8,128)}) custom-call(bf16[2,16,72,128]{3,2,1,0:T(8,128)(2,1)} %get-tuple-element.11.g_ref, f32[18,64]{1,0:T(8,128)} %get-tuple-element.12.first_in, f32[18,64]{1,0:T(8,128)} %get-tuple-element.13.second_in), custom_call_target="tpu_custom_call" | custom-call | tf_op jit(solution)/shard_map/unpack/pallas_call | solution.py:395
